TPU v7x, 128 devices: a whole 4x4x4 slice. The times are simulated.
128 devices in a mesh: grp: 2 (over y_hi), dev: 64 (over x, z, y_lo, core).
Axes of the slice: x: 4, y: 4 (y_hi: 2, y_lo: 2; y = y_hi * 2 + y_lo), z: 4, core: 2. Of those that a mesh axis runs over, the one named last changes fastest.
Arguments:
- multipoles: float32 [2, 384, 41472], P(None, ('grp', 'dev')), may hold values from -6 to 6
- derivatives: float32 [384, 512, 289], P(None, ('grp', 'dev')), may hold values from -0.6666667 to 0.6666667
Outputs:
- taylors: float32 [2, 384, 41472], P(None, ('grp', 'dev'))
All inputs are finite; a program needn't handle non-finite values.
Results may differ from a plain program's by a relative error of at most 0.0001.
Values sent between devices are 32-bit elements; how exact they have to be, the bound alone decides.
A program may use at most 192 MiB of HBM per device.

v0:
```python
import math
import jax
import jax.numpy as jnp
import numpy as np
from jax import lax
from jax.sharding import PartitionSpec as P

ORDER = 8


def reduced_terms(highest):
    listed = []
    for total in range(highest + 1):
        for upper in range(min(total, 1) + 1):
            for first in range(total - upper, -1, -1):
                listed.append((first, total - upper - first, upper))
    return listed


def coupling_matrix(order):
    lower = reduced_terms(order)
    higher = reduced_terms(2 * order)
    where = {}
    for place, triple in enumerate(higher):
        where[triple] = place
    count = len(lower)
    table = np.zeros((len(higher), count * count), np.float32)
    for left, one in enumerate(lower):
        for right, other in enumerate(lower):
            summed = (one[0] + other[0], one[1] + other[1], one[2] + other[2])
            column = left * count + right
            if summed[2] <= 1:
                table[where[summed], column] += 1.0
            else:
                table[where[summed[0] + 2, summed[1], 0], column] -= 1.0
                table[where[summed[0], summed[1] + 2, 0], column] -= 1.0
    return table


def dft_tables(length, positions):
    kvalues = jnp.arange(length, dtype=jnp.int32)
    phase = kvalues[:, None] * positions[None, :] % length
    angle = 2.0 * math.pi / length * phase.astype(jnp.float32)
    factor = 1.0 / math.sqrt(length)
    cosine = jnp.cos(angle) * factor
    sine = jnp.sin(angle) * factor
    forward = jnp.stack([jnp.stack([cosine, sine], 1), jnp.stack([-sine, cosine], 1)], 0)
    inverse = jnp.stack([jnp.stack([cosine.T, -sine.T], 1), jnp.stack([sine.T, cosine.T], 1)], 0)
    return (forward, inverse)


def contract_rows(deriv_rows, spectrum, comp_count):
    table = jnp.asarray(coupling_matrix(ORDER))
    total = deriv_rows.shape[0]
    width = math.gcd(total, 768)
    count = total // width

    def step(index, result):
        start = (index * width).astype(jnp.int32)
        deriv_block = lax.dynamic_slice_in_dim(deriv_rows, start, width, 0)
        coupling = jnp.dot(deriv_block, table, precision=lax.Precision.HIGHEST)
        coupling = coupling.reshape(width, comp_count, comp_count)
        moment_block = lax.dynamic_slice_in_dim(spectrum, start, width, 1)
        block_out = jnp.einsum(
            "pab,rpb->rpa", coupling, moment_block, precision=lax.Precision.HIGHEST
        )
        return lax.dynamic_update_slice_in_dim(result, block_out, start, 1)

    return lax.fori_loop(0, count, step, jnp.zeros(spectrum.shape, spectrum.dtype))


def convolve_group(multipoles, derivatives):
    outer = lax.axis_size("grp")
    inner = lax.axis_size("dev")
    local_rows = multipoles.shape[1]
    length = local_rows * outer * inner
    comp_count = (ORDER + 1) ** 2
    deriv_count = derivatives.shape[2]
    mode_count = derivatives.shape[1]
    row_index = jnp.arange(length, dtype=jnp.int32)
    slab_rows = lax.all_to_all(multipoles, ("grp", "dev"), split_axis=2, concat_axis=1, tiled=True)
    forward, inverse = dft_tables(length, row_index)
    forward_matrix = forward.reshape(2 * length, 2 * length)
    inverse_matrix = inverse.reshape(2 * length, 2 * length)
    matrix = slab_rows.reshape(2 * length, mode_count * comp_count)
    spectrum = jnp.dot(forward_matrix, matrix, precision=lax.Precision.HIGHEST)
    spectrum = spectrum.reshape(2, length * mode_count, comp_count)
    deriv_rows = derivatives.reshape(length * mode_count, deriv_count)
    taylor_k = contract_rows(deriv_rows, spectrum, comp_count)
    taylor_k = taylor_k.reshape(2 * length, mode_count * comp_count)
    returned = jnp.dot(inverse_matrix, taylor_k, precision=lax.Precision.HIGHEST)
    returned = returned.reshape(2, length, mode_count * comp_count)
    result = lax.all_to_all(returned, ("grp", "dev"), split_axis=1, concat_axis=2, tiled=True)
    return result


def on_device(multipoles, derivatives):
    return convolve_group(multipoles, derivatives)


def solution(mesh):
    in_specs = (P(None, ("grp", "dev"), None), P(None, ("grp", "dev"), None))
    out_specs = P(None, ("grp", "dev"), None)
    return jax.shard_map(
        on_device, mesh=mesh, in_specs=in_specs, out_specs=out_specs, check_vma=False
    )
```

profile of v0, /device:TPU:0, one launch (start us, length us, event | category | flops | bytes accessed | tf_op | source)
XLA Modules:
  0.0 560.5 jit_solution(2674592462002672816)
XLA Ops:
  0.0 40.9 %copy.55 = f32[2,3,41472]{1,0,2:T(2,128)} copy(f32[2,3,41472]{2,0,1:T(2,128)} %param.5) | data formatting | bytes 1990656 | tf_op args[0]
  40.9 48.3 %reshape.123 = f32[128,1,1944]{2,1,0:T(1,128)} reshape(f32[41472,2,3]{2,1,0:T(2,128)} %bitcast.37) | data formatting | bytes 1990656
  89.2 11.9 %all-to-all-start = ((f32[128,1,1944]{2,1,0:T(1,128)}), f32[128,1,1944]{2,1,0:T(1,128)}, u32[]{:S(2)}, u32[]{:S(2)}) async-start(f32[128,1,1944]{2,1,0:T(1,128)} %reshape.123), calls=%async_computation | async-start | bytes 2097152 | tf_op jit(solution)/shard_map/all_to_all | solution.py:81
  101.1 2.3 fusion.16
  103.3 2.4 sine_multiply_fusion
  105.8 1.3 fusion.9
  107.1 1.4 copy.51
  108.5 2.7 copy.53
  111.2 0.4 copy.50
  111.6 1.4 copy.52
  113.0 0.2 pad_maximum_fusion
  113.1 1.8 copy.54
  115.0 0.0 copy-start.5
  115.0 1.6 copy.72
  116.6 0.7 copy-done.5
  117.3 2.5 copy.59
  119.8 3.1 reshape.118
  122.9 0.6 broadcast.157
  123.5 4.3 reduce
  127.8 53.6 %reshape.124 = f32[41472,2,3]{2,1,0:T(2,128)} reshape(f32[128,1944]{1,0:T(8,128)S(1)} %reduce) | data formatting | bytes 1990656
  181.5 38.0 %copy.67 = f32[2,3,128,324]{3,2,0,1:T(8,128)S(1)} copy(f32[2,3,128,324]{1,0,3,2:T(2,128)} %bitcast.38) | data formatting | bytes 1990656 | tf_op jit(solution)/shard_map/all_to_all | solution.py:81
  219.5 2.0 copy.57
  221.5 1.8 reshape.116
  223.2 6.6 %fusion.18 = f32[768,324]{1,0:T(8,128)} fusion(f32[768,768]{1,0:T(8,128)} %bitcast.39, f32[768,324]{1,0:T(8,128)S(1)} %reshape.116), kind=kOutput, calls=%fused_computation.30 | convolution fusion | flops 2293235712 | bytes 4349952 | tf_op jit(solution)/shard_map/dot_general | solution.py:86
  229.8 2.6 reshape.117
  232.5 1.3 broadcast_in_dim.2.clone
  233.7 285.8 %while.14 = (s32[]{:T(128)}, f32[2,1536,81]{2,1,0:T(8,128)}, f32[2,1536,81]{2,1,0:T(8,128)}, f32[1536,289]{1,0:T(8,128)S(1)}, s32[]{:T(128)}, /*index=5*/s32[]{:T(128)}, s32[]{:T(128)}, s32[]{:T(128)}, f32[289,6561]{1,0:T(8,128)}) while((s32[]{:T(128)}, f32[2,1536,81]{2,1,0:T(8,128)}, f32[2,1536,81]{2,1,0:T(8,128)}, ...), condition=%wide.region_1.2_spmd.clone, body=%wide.region_0.1_spmd.sunk.clone.sunk | while | flops 17595656192 | bytes 141222864 | solution.py:69
  233.9 37.5 %fusion.32 = f32[768,6561]{0,1:T(8,128)} fusion(f32[289,6561]{1,0:T(8,128)} %get-tuple-element.202, f32[1536,289]{1,0:T(8,128)S(1)} %get-tuple-element.197, s32[]{:T(128)S(6)} %select_n.65), kind=kOutput, calls=%fused_computation.1.clone.1 | convolution fusion | flops 17474723840 | bytes 28919560 | tf_op jit(solution)/shard_map/while/body/eval_jaxpr/dot_general | solution.py:61
  271.4 17.5 %reshape.126 = f32[768,81,81]{0,2,1:T(8,128)} reshape(f32[768,6561]{0,1:T(8,128)} %fusion.32) | data formatting | bytes 40310784 | tf_op jit(solution)/shard_map/while/body/eval_jaxpr/reshape | solution.py:62
  288.8 27.8 %copy.81 = f32[768,81,81]{2,1,0:T(8,128)} copy(f32[768,81,81]{0,2,1:T(8,128)} %reshape.126) | data formatting | bytes 40310784 | tf_op jit(solution)/shard_map/while/body/eval_jaxpr/reshape | solution.py:62
  316.6 1.2 constant_dynamic-slice_fusion.2
  317.8 57.5 %convolution_bitcast_fusion.2 = f32[2,768,81]{2,0,1:T(2,128)S(1)} fusion(f32[768,81,81]{2,1,0:T(8,128)} %copy.81, f32[2,768,81]{2,1,0:T(8,128)S(1)} %constant_dynamic-slice_fusion.2), kind=kOutput, calls=%fused_computation.clone.1 | convolution fusion | flops 120932352 | bytes 21150720 | tf_op jit(solution)/shard_map/while/body/eval_jaxpr/pab,rpb->rpa/dot_general | solution.py:64
  375.4 0.1 copy_dynamic-update-slice_fusion.2
  375.5 1.2 copy-done.1
  376.7 37.4 %fusion.32 = f32[768,6561]{0,1:T(8,128)} fusion(f32[289,6561]{1,0:T(8,128)} %get-tuple-element.202, f32[1536,289]{1,0:T(8,128)S(1)} %get-tuple-element.197, s32[]{:T(128)S(6)} %select_n.65), kind=kOutput, calls=%fused_computation.1.clone.1 | convolution fusion | flops 17474723840 | bytes 28919560 | tf_op jit(solution)/shard_map/while/body/eval_jaxpr/dot_general | solution.py:61
  414.1 17.5 %reshape.126 = f32[768,81,81]{0,2,1:T(8,128)} reshape(f32[768,6561]{0,1:T(8,128)} %fusion.32) | data formatting | bytes 40310784 | tf_op jit(solution)/shard_map/while/body/eval_jaxpr/reshape | solution.py:62
  431.6 27.8 %copy.81 = f32[768,81,81]{2,1,0:T(8,128)} copy(f32[768,81,81]{0,2,1:T(8,128)} %reshape.126) | data formatting | bytes 40310784 | tf_op jit(solution)/shard_map/while/body/eval_jaxpr/reshape | solution.py:62
  459.4 1.2 constant_dynamic-slice_fusion.2
  460.6 57.5 %convolution_bitcast_fusion.2 = f32[2,768,81]{2,0,1:T(2,128)S(1)} fusion(f32[768,81,81]{2,1,0:T(8,128)} %copy.81, f32[2,768,81]{2,1,0:T(8,128)S(1)} %constant_dynamic-slice_fusion.2), kind=kOutput, calls=%fused_computation.clone.1 | convolution fusion | flops 120932352 | bytes 21150720 | tf_op jit(solution)/shard_map/while/body/eval_jaxpr/pab,rpb->rpa/dot_general | solution.py:64
  518.1 0.1 copy_dynamic-update-slice_fusion.2
  518.2 1.2 copy-done.1
  519.6 2.0 reshape.119
  521.6 0.1 copy-done.4
  521.7 3.7 fusion.4
  525.4 2.4 copy.63
  527.8 30.1 %all_to_all.33 = f32[2,384,324]{2,0,1:T(2,128)S(1)} all-to-all(f32[2,384,324]{2,0,1:T(2,128)S(1)} %copy.63), channel_id=1, replica_groups=mesh['grp'=2,'dev'=64] {'grp','dev'}, dimensions={1} | all-to-all | bytes 1990656 | tf_op jit(solution)/shard_map/all_to_all | solution.py:93
  557.8 0.1 copy.64
  557.9 2.4 all_to_all.30
  (12 shorter events, 0.0 us)
Async XLA Ops:
  89.2 33.7 %all-to-all-start = ((f32[128,1,1944]{2,1,0:T(1,128)}), f32[128,1,1944]{2,1,0:T(1,128)}, u32[]{:S(2)}, u32[]{:S(2)}) async-start(f32[128,1,1944]{2,1,0:T(1,128)} %reshape.123), calls=%async_computation | async-start | bytes 2097152 | tf_op jit(solution)/shard_map/all_to_all | solution.py:81
  111.6 1.4 copy-start.2
  115.0 2.3 copy-start.5
  317.8 57.6 %copy-start = (f32[2,1536,81]{2,1,0:T(8,128)S(1)}, f32[2,1536,81]{2,1,0:T(8,128)}, u32[]{:S(2)}) copy-start(f32[2,1536,81]{2,1,0:T(8,128)} %get-tuple-element.186) | copy-start | bytes 2985988 | tf_op jit(solution)/shard_map/while
  375.5 1.2 copy-start.1
  460.6 57.6 %copy-start = (f32[2,1536,81]{2,1,0:T(8,128)S(1)}, f32[2,1536,81]{2,1,0:T(8,128)}, u32[]{:S(2)}) copy-start(f32[2,1536,81]{2,1,0:T(8,128)} %get-tuple-element.186) | copy-start | bytes 2985988 | tf_op jit(solution)/shard_map/while
  518.2 1.2 copy-start.1
  519.6 2.0 copy-start.3
  519.6 2.1 copy-start.4
where the time goes:
time: 570 us; the launch traced here: 561 us
  local copies, waits for them, and re-layouts  307 us (54%)
  matrix products  200 us (35%)
  blocking collectives  30.1 us (5%)
  starting transfers between devices  11.9 us (2%)
  other arithmetic  10.5 us (2%)
    unnamed x13, local copies, waits for them, and re-layouts  148 us
    dot_general x2, matrix products, step(): jnp.einsum('pab,rpb->rpa', coupling, moment_block, precision=lax.Precisio...  115 us
    reshape x4, local copies, waits for them, and re-layouts, step(): coupling = coupling.reshape(width, comp_count, comp_count)  90.5 us
    dot_general x2, matrix products, step(): coupling = jnp.dot(deriv_block, table, precision=lax.Precision.HIGHEST)  74.9 us
    all_to_all x3, local copies, waits for them, and re-layouts, convolve_group(): lax.all_to_all(multipoles, ('grp', 'dev'), split_axis=2, concat_axis=1, t...  40.6 us
    all_to_all x1, blocking collectives, convolve_group(): lax.all_to_all(returned, ('grp', 'dev'), split_axis=1, concat_axis=2, til...  30.1 us
    all_to_all x1, starting transfers between devices, convolve_group(): lax.all_to_all(multipoles, ('grp', 'dev'), split_axis=2, concat_axis=1, t...  11.9 us
  transfers between devices with their start and end apart: 1, of which 0 were waited for; matrix products, arithmetic and copies ran while one was open for 4% of the time, Pallas kernels for 0%

commit v1 on v0

--- a/solution.py
+++ b/solution.py
@@ -6,6 +6,15 @@
 from jax.sharding import PartitionSpec as P
 
 ORDER = 8
+
+
+def _keep_up_pages(message, named_axis):
+    return jnp.concatenate(
+        lax.all_to_all(
+            jnp.stack(jnp.split(message, lax.axis_size(named_axis), 2)), named_axis, 0, 0
+        ),
+        1,
+    )
 
 
 def reduced_terms(highest):
@@ -78,7 +87,7 @@
     deriv_count = derivatives.shape[2]
     mode_count = derivatives.shape[1]
     row_index = jnp.arange(length, dtype=jnp.int32)
-    slab_rows = lax.all_to_all(multipoles, ("grp", "dev"), split_axis=2, concat_axis=1, tiled=True)
+    slab_rows = _keep_up_pages(multipoles, ("grp", "dev"))
     forward, inverse = dft_tables(length, row_index)
     forward_matrix = forward.reshape(2 * length, 2 * length)
     inverse_matrix = inverse.reshape(2 * length, 2 * length)

time: 570 us -> 514 us (0.902)
  local copies, waits for them, and re-layouts: 307 us -> 257 us
    all_to_all x3 -> x0, local copies, waits for them, and re-layouts: 40.6 us -> none  [convolve_group(): lax.all_to_all(multipoles, ('grp', 'dev'), split_axis=2, concat_axis=1, t...]
    unnamed x13 -> x139, local copies, waits for them, and re-layouts: 148 us -> 136 us
where the time goes in v1:
time: 514 us; the launch traced here: 506 us
  local copies, waits for them, and re-layouts  257 us (50%)
  matrix products  200 us (39%)
  blocking collectives  30.1 us (6%)
  starting transfers between devices  11.8 us (2%)
  other arithmetic  6.16 us (1%)
    unnamed x139, local copies, waits for them, and re-layouts  136 us
    dot_general x2, matrix products, step(): jnp.einsum('pab,rpb->rpa', coupling, moment_block, precision=lax.Precisio...  115 us
    reshape x4, local copies, waits for them, and re-layouts, step(): coupling = coupling.reshape(width, comp_count, comp_count)  90.4 us
    dot_general x2, matrix products, step(): coupling = jnp.dot(deriv_block, table, precision=lax.Precision.HIGHEST)  74.9 us
    all_to_all x1, blocking collectives, convolve_group(): lax.all_to_all(returned, ('grp', 'dev'), split_axis=1, concat_axis=2, til...  30.1 us
    all_to_all x1, starting transfers between devices, _keep_up_pages(): lax.all_to_all(jnp.stack(jnp.split(message, lax.axis_size(named_axis), 2)...  11.8 us
  transfers between devices with their start and end apart: 1, of which 0 were waited for; matrix products, arithmetic and copies ran while one was open for 4% of the time, Pallas kernels for 0%

profile of v1, /device:TPU:0, one launch (start us, length us, event | category | flops | bytes accessed | tf_op | source)
XLA Modules:
  0.0 506.4 jit_solution(17329579955231167222)
XLA Ops:
  0.0 1.4 constant_dynamic-update-slice_fusion.127
  1.4 1.4 constant_dynamic-update-slice_fusion.126
  2.8 1.4 constant_dynamic-update-slice_fusion.125
  4.2 1.4 constant_dynamic-update-slice_fusion.124
  6.9 1.4 constant_dynamic-update-slice_fusion.122
  8.3 1.4 constant_dynamic-update-slice_fusion.121
  9.7 1.4 constant_dynamic-update-slice_fusion.120
  15.2 1.4 constant_dynamic-update-slice_fusion.116
  16.6 1.4 constant_dynamic-update-slice_fusion.115
  29.0 1.4 constant_dynamic-update-slice_fusion.106
  37.3 1.4 constant_dynamic-update-slice_fusion.100
  38.7 1.4 constant_dynamic-update-slice_fusion.99
  52.4 1.4 constant_dynamic-update-slice_fusion.89
  56.5 1.4 constant_dynamic-update-slice_fusion.86
  57.9 1.4 constant_dynamic-update-slice_fusion.85
  64.8 1.4 constant_dynamic-update-slice_fusion.80
  73.1 1.4 constant_dynamic-update-slice_fusion.74
  74.5 1.4 constant_dynamic-update-slice_fusion.73
  78.6 1.4 constant_dynamic-update-slice_fusion.70
  82.8 1.4 constant_dynamic-update-slice_fusion.67
  85.5 1.4 constant_dynamic-update-slice_fusion.65
  131.3 11.8 %all-to-all-start = ((f32[128,2,3,324]{3,1,2,0:T(2,128)}), f32[128,2,3,324]{3,1,2,0:T(2,128)}, u32[]{:S(2)}, u32[]{:S(2)}) async-start(f32[128,2,3,324]{3,1,2,0:T(2,128)} %constant_dynamic-update-slice_fusion), calls=%async_computation | async-start | bytes 2359296 | tf_op jit(solution)/shard_map/all_to_all | solution.py:13
  143.2 2.3 fusion.16
  145.4 2.4 sine_multiply_fusion
  149.2 1.4 copy.36
  150.6 2.7 copy.38
  155.2 1.8 copy.39
  157.0 1.6 copy.54
  159.4 2.5 copy.42
  161.9 2.7 reshape.117
  164.6 2.8 copy.40
  167.4 1.8 reshape_reshape.3
  169.1 6.6 %fusion.18 = f32[768,324]{1,0:T(8,128)} fusion(f32[768,768]{1,0:T(8,128)} %bitcast.290, f32[768,324]{1,0:T(8,128)S(1)} %reshape_reshape.3), kind=kOutput, calls=%fused_computation.158 | convolution fusion | flops 2293235712 | bytes 4349952 | tf_op jit(solution)/shard_map/dot_general | solution.py:95
  175.7 2.6 reshape.116
  179.6 285.9 %while.14 = (s32[]{:T(128)}, f32[2,1536,81]{2,1,0:T(8,128)}, f32[2,1536,81]{2,1,0:T(8,128)}, f32[1536,289]{1,0:T(8,128)S(1)}, s32[]{:T(128)}, /*index=5*/s32[]{:T(128)}, s32[]{:T(128)}, s32[]{:T(128)}, f32[289,6561]{1,0:T(8,128)}) while((s32[]{:T(128)}, f32[2,1536,81]{2,1,0:T(8,128)}, f32[2,1536,81]{2,1,0:T(8,128)}, ...), condition=%wide.region_1.2_spmd.clone, body=%wide.region_0.1_spmd.sunk.clone.sunk | while | flops 17595656192 | bytes 141222864 | solution.py:78
  180.0 37.5 %fusion.32 = f32[768,6561]{0,1:T(8,128)} fusion(f32[289,6561]{1,0:T(8,128)} %get-tuple-element.198, f32[1536,289]{1,0:T(8,128)S(1)} %get-tuple-element.193, s32[]{:T(128)S(6)} %select_n.65), kind=kOutput, calls=%fused_computation.1.clone.1 | convolution fusion | flops 17474723840 | bytes 28919560 | tf_op jit(solution)/shard_map/while/body/eval_jaxpr/dot_general | solution.py:70
  217.5 17.5 %reshape.123 = f32[768,81,81]{0,2,1:T(8,128)} reshape(f32[768,6561]{0,1:T(8,128)} %fusion.32) | data formatting | bytes 40310784 | tf_op jit(solution)/shard_map/while/body/eval_jaxpr/reshape | solution.py:71
  234.9 27.7 %copy.63 = f32[768,81,81]{2,1,0:T(8,128)} copy(f32[768,81,81]{0,2,1:T(8,128)} %reshape.123) | data formatting | bytes 40310784 | tf_op jit(solution)/shard_map/while/body/eval_jaxpr/reshape | solution.py:71
  263.8 57.5 %convolution_bitcast_fusion.2 = f32[2,768,81]{2,0,1:T(2,128)S(1)} fusion(f32[768,81,81]{2,1,0:T(8,128)} %copy.63, f32[2,768,81]{2,1,0:T(8,128)S(1)} %constant_dynamic-slice_fusion.2), kind=kOutput, calls=%fused_computation.clone.1 | convolution fusion | flops 120932352 | bytes 21150720 | tf_op jit(solution)/shard_map/while/body/eval_jaxpr/pab,rpb->rpa/dot_general | solution.py:73
  322.7 37.5 %fusion.32 = f32[768,6561]{0,1:T(8,128)} fusion(f32[289,6561]{1,0:T(8,128)} %get-tuple-element.198, f32[1536,289]{1,0:T(8,128)S(1)} %get-tuple-element.193, s32[]{:T(128)S(6)} %select_n.65), kind=kOutput, calls=%fused_computation.1.clone.1 | convolution fusion | flops 17474723840 | bytes 28919560 | tf_op jit(solution)/shard_map/while/body/eval_jaxpr/dot_general | solution.py:70
  360.1 17.5 %reshape.123 = f32[768,81,81]{0,2,1:T(8,128)} reshape(f32[768,6561]{0,1:T(8,128)} %fusion.32) | data formatting | bytes 40310784 | tf_op jit(solution)/shard_map/while/body/eval_jaxpr/reshape | solution.py:71
  377.6 27.7 %copy.63 = f32[768,81,81]{2,1,0:T(8,128)} copy(f32[768,81,81]{0,2,1:T(8,128)} %reshape.123) | data formatting | bytes 40310784 | tf_op jit(solution)/shard_map/while/body/eval_jaxpr/reshape | solution.py:71
  406.5 57.5 %convolution_bitcast_fusion.2 = f32[2,768,81]{2,0,1:T(2,128)S(1)} fusion(f32[768,81,81]{2,1,0:T(8,128)} %copy.63, f32[2,768,81]{2,1,0:T(8,128)S(1)} %constant_dynamic-slice_fusion.2), kind=kOutput, calls=%fused_computation.clone.1 | convolution fusion | flops 120932352 | bytes 21150720 | tf_op jit(solution)/shard_map/while/body/eval_jaxpr/pab,rpb->rpa/dot_general | solution.py:73
  465.5 2.0 reshape.118
  467.6 3.7 fusion.4
  471.3 2.4 copy.46
  473.7 30.1 %all_to_all.23 = f32[2,384,324]{2,0,1:T(2,128)S(1)} all-to-all(f32[2,384,324]{2,0,1:T(2,128)S(1)} %copy.46), channel_id=1, replica_groups=mesh['grp'=2,'dev'=64] {'grp','dev'}, dimensions={1} | all-to-all | bytes 1990656 | tf_op jit(solution)/shard_map/all_to_all | solution.py:102
  503.8 2.4 all_to_all.20
  (136 shorter events, 112.5 us)
Async XLA Ops:
  0.0 88.3 %copy-start.6 = (f32[2,3,41472]{2,0,1:T(2,128)S(1)}, f32[2,3,41472]{2,0,1:T(2,128)}, u32[]{:S(2)}) copy-start(f32[2,3,41472]{2,0,1:T(2,128)} %param.5) | copy-start | bytes 2985988
  131.3 33.2 %all-to-all-start = ((f32[128,2,3,324]{3,1,2,0:T(2,128)}), f32[128,2,3,324]{3,1,2,0:T(2,128)}, u32[]{:S(2)}, u32[]{:S(2)}) async-start(f32[128,2,3,324]{3,1,2,0:T(2,128)} %constant_dynamic-update-slice_fusion), calls=%async_computation | async-start | bytes 2359296 | tf_op jit(solution)/shard_map/all_to_all | solution.py:13
  153.7 1.4 copy-start.2
  157.0 2.3 copy-start.5
  263.8 57.6 %copy-start = (f32[2,1536,81]{2,1,0:T(8,128)S(1)}, f32[2,1536,81]{2,1,0:T(8,128)}, u32[]{:S(2)}) copy-start(f32[2,1536,81]{2,1,0:T(8,128)} %get-tuple-element.182) | copy-start | bytes 2985988 | tf_op jit(solution)/shard_map/while
  321.5 1.2 copy-start.1
  406.5 57.6 %copy-start = (f32[2,1536,81]{2,1,0:T(8,128)S(1)}, f32[2,1536,81]{2,1,0:T(8,128)}, u32[]{:S(2)}) copy-start(f32[2,1536,81]{2,1,0:T(8,128)} %get-tuple-element.182) | copy-start | bytes 2985988 | tf_op jit(solution)/shard_map/while
  464.2 1.2 copy-start.1
  465.5 2.0 copy-start.3
  465.5 2.1 copy-start.4
